TPU v7x, 256 devices: a whole 4x4x8 slice. The times are simulated.
256 devices in a mesh: seq: 32 (over z, x), blk: 8 (over y, core).
Axes of the slice: x: 4, y: 4, z: 8, core: 2. Of those that a mesh axis runs over, the one named last changes fastest.
Arguments:
- qkv: bfloat16 [32768, 12288], P(('seq', 'blk')), may hold values from -24 to 24
- kept_kv: bfloat16 [32, 2, 128, 4096], P('blk', None, None, 'seq'), may hold values from -24 to 24
- cur_list: int32 [256, 8], replicated, may hold values from 0 to 255, as said below
- kept_list: int32 [256, 12], replicated, may hold values from 0 to 31, as said below
- kept_count: int32 [256], replicated, may hold values from 1 to 12, as said below
Outputs:
- attn_out: bfloat16 [32768, 4096], P(('seq', 'blk'))
Inputs may be any that keep to these rules, and one draw needn't show every extreme that they name: `cur_list`: row t lists 8 different tiles t2 of tile t's spatial region, that is with (t2) % 8 equal to (t) % 8; the first entry is t itself. `kept_list`: each row names 12 different kept blocks. `kept_count`: some tile uses all 12 slots.
All inputs are finite; a program needn't handle non-finite values.
Results may differ from a plain program's by a relative error of at most 0.0025.
Values may be sent and summed in bfloat16 or wider, within the bound.
A program may use at most 64 MiB of HBM per device.

v0:
```python
import math

import jax
import jax.numpy as jnp
from jax import lax
from jax.sharding import PartitionSpec as P

HEAD_DIM = 128


MASKED_SCORE = -1e30


def per_device(qkv, kept_kv, cur_list, kept_list, kept_count):
    seq_count = lax.axis_size("seq")
    blk_count = lax.axis_size("blk")
    tok_rows = qkv.shape[0]
    head_width = HEAD_DIM
    head_total = qkv.shape[1] // (3 * head_width)
    tile_len = kept_kv.shape[2]
    tiles_dev = tok_rows // tile_len
    shaped = qkv.reshape(tok_rows, 3, head_total, head_width)
    arrived = lax.all_to_all(shaped, "seq", split_axis=2, concat_axis=0, tiled=True)
    head_dev = arrived.shape[2]
    tile_mine = seq_count * tiles_dev
    grouped = arrived.reshape(tile_mine, tile_len, 3, head_dev, head_width)
    ordered = jnp.transpose(grouped, (2, 0, 3, 1, 4))
    queries_all = ordered[0]
    near_keys_all = ordered[1]
    near_values_all = ordered[2]
    kept_all = lax.all_gather(kept_kv, "blk", axis=0, tiled=True)
    kept_all = jnp.transpose(
        kept_all.reshape(kept_all.shape[0], 2, tile_len, head_dev, head_width), (0, 1, 3, 2, 4)
    )
    far_keys_all = kept_all[:, 0]
    far_values_all = kept_all[:, 1]
    region = lax.axis_index("blk")
    local_ids = jnp.arange(tile_mine, dtype=jnp.int32)
    tile_ids = (local_ids // tiles_dev * blk_count + region) * tiles_dev + local_ids % tiles_dev
    cur_ids = cur_list[tile_ids]
    cur_local = cur_ids // tiles_dev // blk_count * tiles_dev + cur_ids % tiles_dev
    kept_ids = kept_list[tile_ids]
    slot_counts = kept_count[tile_ids]
    score_scale = 1.0 / math.sqrt(head_width)
    window_slots = kept_ids.shape[1]
    near_count = cur_local.shape[1]
    tiles_step = 4
    step_total = tile_mine // tiles_step

    def attend(pieces):
        queries, cur_sel, kept_sel, slot_count = pieces
        near_keys = near_keys_all[cur_sel]
        near_values = near_values_all[cur_sel]
        near_scores = (
            jnp.einsum("bhid,bnhkd->bhink", queries, near_keys, preferred_element_type=jnp.float32)
            * score_scale
        )
        near_max = near_scores.max(axis=(3, 4))[..., None, None]
        far_keys = far_keys_all[kept_sel]
        far_values = far_values_all[kept_sel]
        far_scores = (
            jnp.einsum("bhid,bwhkd->bhiwk", queries, far_keys, preferred_element_type=jnp.float32)
            * score_scale
        )
        is_live = (jnp.arange(window_slots)[None, :] < slot_count[:, None])[:, None, None, :, None]
        far_scores = jnp.where(is_live, far_scores, MASKED_SCORE)
        row_max = jnp.maximum(near_max, far_scores.max(axis=(3, 4))[..., None, None])
        near_weights = jnp.exp(near_scores - row_max)
        far_weights = jnp.where(is_live, jnp.exp(far_scores - row_max), 0.0)
        row_total = near_weights.sum(axis=(3, 4)) + far_weights.sum(axis=(3, 4))
        mixture = jnp.einsum(
            "bhink,bnhkd->bhid",
            near_weights.astype(jnp.bfloat16),
            near_values,
            preferred_element_type=jnp.float32,
        )
        mixture = mixture + jnp.einsum(
            "bhiwk,bwhkd->bhid",
            far_weights.astype(jnp.bfloat16),
            far_values,
            preferred_element_type=jnp.float32,
        )
        result_rows = (mixture / row_total[..., None]).astype(jnp.bfloat16)
        return jnp.transpose(result_rows, (0, 2, 1, 3))

    attended = lax.map(
        attend,
        (
            queries_all.reshape(step_total, tiles_step, head_dev, tile_len, head_width),
            cur_local.reshape(step_total, tiles_step, near_count),
            kept_ids.reshape(step_total, tiles_step, window_slots),
            slot_counts.reshape(step_total, tiles_step),
        ),
    )
    attended = attended.reshape(seq_count * tok_rows, head_dev, head_width)
    returned = lax.all_to_all(attended, "seq", split_axis=0, concat_axis=1, tiled=True)
    return returned.reshape(tok_rows, head_total * head_width)


def solution(mesh):
    placed = (P(("seq", "blk"), None), P("blk", None, None, "seq"), P(), P(), P())
    return jax.shard_map(
        per_device, mesh=mesh, in_specs=placed, out_specs=P(("seq", "blk"), None), check_vma=False
    )
```

profile of v0, /device:TPU:2, one launch (start us, length us, event | category | flops | bytes accessed | tf_op | source)
XLA Modules:
  0.0 308.9 jit_solution(16223919463636740690)
XLA Ops:
  6.5 3.5 %copy.45 = bf16[128,12288]{0,1:T(8,128)(2,1)S(1)} copy(bf16[128,12288]{1,0:T(8,128)(2,1)} %param.7) | data formatting | bytes 6291456 | tf_op args[0]
  11.9 11.7 %all-to-all-start = ((bf16[128,3,32,128]{0,3,1,2:T(8,128)(2,1)}), bf16[128,3,32,128]{0,3,1,2:T(8,128)(2,1)S(1)}, u32[]{:S(2)}, u32[]{:S(2)}) async-start(bf16[128,3,32,128]{0,3,1,2:T(8,128)(2,1)} %copy.46), calls=%async_computation | async-start | bytes 6291456 | tf_op jit(solution)/shard_map/all_to_all | solution.py:23
  26.8 28.6 %all-gather.2.cloned.1.call-done = bf16[32,2,128,128]{3,2,0,1:T(8,128)(2,1)} async-done(((bf16[4,2,128,128]{3,2,0,1:T(8,128)(2,1)}), bf16[32,2,128,128]{3,2,0,1:T(8,128)(2,1)}) %all-gather.2.cloned.1.call-update) | async-done | bytes 2097168 | tf_op jit(solution)/shard_map/all_gather | solution.py:31
  55.4 3.1 %slice_bitcast_fusion = (bf16[32,1,128,128]{3,2,1,0:T(8,128)(2,1)}, bf16[32,1,128,128]{3,2,1,0:T(8,128)(2,1)}) fusion(bf16[32,2,1,128,128]{4,3,0,2,1:T(8,128)(2,1)} %bitcast.130), kind=kLoop, calls=%fused_computation.46 | loop fusion | bytes 4194304 | tf_op jit(solution)/shard_map/squeeze | solution.py:36
  58.5 36.5 %all-to-all-done = bf16[128,3,32,128]{0,3,1,2:T(8,128)(2,1)S(1)} async-done(((bf16[128,3,32,128]{0,3,1,2:T(8,128)(2,1)}), bf16[128,3,32,128]{0,3,1,2:T(8,128)(2,1)S(1)}, u32[]{:S(2)}, u32[]{:S(2)}) %all-to-all-start) | async-done | bytes 3145760 | tf_op jit(solution)/shard_map/all_to_all | solution.py:23
  96.7 2.3 copy.51
  100.3 160.1 %while.10 = (s32[]{:T(128)}, bf16[8,4,128,1,128]{4,2,1,3,0:T(8,128)(2,1)}, bf16[8,4,1,128,128]{3,4,1,0,2:T(8,128)(2,1)}, s32[8,4,8]{2,1,0:T(4,128)S(1)}, bf16[32...) while((s32[]{:T(128)}, ...), condition=%wide.region_5.6_spmd, body=%wide.region_0.5_spmd.sunk | while | flops 685704448 | bytes 57583712 | solution.py:86
  100.4 2.1 gather_fusion.2
  102.6 3.1 %fusion.67 = (f32[4,128]{1,0:T(4,128)S(1)}, f32[4,128,12,128]{1,3,2,0:T(8,128)}) fusion(pred[4,12]{1,0:T(4,128)(4,1)S(1)} %iota_compare_fusion.2, bf16[4,12,128,128]{3,2,1,0:T(8,128)(2,1)S(1)} %bitcast.120, bf16[8,4,1,128,128]{3,4,1,0,2:T(8,128)(2,1)} %get-tuple-element.220, s32[]{:T(128)} %get-tuple-element.207), kind=kOutput, calls=%fused_computation.9.clone.1 | convolution fusion | flops 203685376 | bytes 4852272 | tf_op jit(solution)/shard_map/while/body/eval_jaxpr/bhid,bwhkd->bhiwk/dot_general | solution.py:62
  111.1 2.0 gather_fusion
  113.7 3.4 %gather_fusion.3 = bf16[48,128,128]{2,1,0:T(8,128)(2,1)} fusion(bf16[32,128,128]{2,1,0:T(8,128)(2,1)} %bitcast.123, s32[1024]{0:T(1024)S(1)} %pad_clamp_fusion.6), kind=kCustom, calls=%fused_computation.3.clone.1 | custom fusion | bytes 3145920 | tf_op jit(solution)/shard_map/while/body/eval_jaxpr/gather | solution.py:60
  117.1 3.2 %fusion.70 = bf16[8,4,128,1,128]{4,2,1,3,0:T(8,128)(2,1)} fusion(bf16[8,4,128,1,128]{4,2,1,3,0:T(8,128)(2,1)} %get-tuple-element.208, s32[]{:T(128)} %get-tuple-element.207, f32[4,128,128]{2,1,0:T(8,128)S(1)} %convolution_bitcast_fusion.2, bf16[4,12,128,128]{3,2,1,0:T(8,128)(2,1)} %bitcast.124, f32[4,128,12,128]{1,3,2,0:T(8,128)S(1)} %copy-done.2, ...), kind=kOutput, calls=%fused_computation.24.clone.1 | convolution fusion | flops 205455360 | bytes 5116464 | tf_op jit(solution)/shard_map/while/body/eval_jaxpr/bhiwk,bwhkd->bhid/dot_general | solution.py:77
  120.4 2.1 gather_fusion.2
  122.6 3.1 %fusion.67 = (f32[4,128]{1,0:T(4,128)S(1)}, f32[4,128,12,128]{1,3,2,0:T(8,128)}) fusion(pred[4,12]{1,0:T(4,128)(4,1)S(1)} %iota_compare_fusion.2, bf16[4,12,128,128]{3,2,1,0:T(8,128)(2,1)S(1)} %bitcast.120, bf16[8,4,1,128,128]{3,4,1,0,2:T(8,128)(2,1)} %get-tuple-element.220, s32[]{:T(128)} %get-tuple-element.207), kind=kOutput, calls=%fused_computation.9.clone.1 | convolution fusion | flops 203685376 | bytes 4852272 | tf_op jit(solution)/shard_map/while/body/eval_jaxpr/bhid,bwhkd->bhiwk/dot_general | solution.py:62
  131.1 2.0 gather_fusion
  133.7 3.4 %gather_fusion.3 = bf16[48,128,128]{2,1,0:T(8,128)(2,1)} fusion(bf16[32,128,128]{2,1,0:T(8,128)(2,1)} %bitcast.123, s32[1024]{0:T(1024)S(1)} %pad_clamp_fusion.6), kind=kCustom, calls=%fused_computation.3.clone.1 | custom fusion | bytes 3145920 | tf_op jit(solution)/shard_map/while/body/eval_jaxpr/gather | solution.py:60
  137.1 3.2 %fusion.70 = bf16[8,4,128,1,128]{4,2,1,3,0:T(8,128)(2,1)} fusion(bf16[8,4,128,1,128]{4,2,1,3,0:T(8,128)(2,1)} %get-tuple-element.208, s32[]{:T(128)} %get-tuple-element.207, f32[4,128,128]{2,1,0:T(8,128)S(1)} %convolution_bitcast_fusion.2, bf16[4,12,128,128]{3,2,1,0:T(8,128)(2,1)} %bitcast.124, f32[4,128,12,128]{1,3,2,0:T(8,128)S(1)} %copy-done.2, ...), kind=kOutput, calls=%fused_computation.24.clone.1 | convolution fusion | flops 205455360 | bytes 5116464 | tf_op jit(solution)/shard_map/while/body/eval_jaxpr/bhiwk,bwhkd->bhid/dot_general | solution.py:77
  140.5 2.1 gather_fusion.2
  142.6 3.1 %fusion.67 = (f32[4,128]{1,0:T(4,128)S(1)}, f32[4,128,12,128]{1,3,2,0:T(8,128)}) fusion(pred[4,12]{1,0:T(4,128)(4,1)S(1)} %iota_compare_fusion.2, bf16[4,12,128,128]{3,2,1,0:T(8,128)(2,1)S(1)} %bitcast.120, bf16[8,4,1,128,128]{3,4,1,0,2:T(8,128)(2,1)} %get-tuple-element.220, s32[]{:T(128)} %get-tuple-element.207), kind=kOutput, calls=%fused_computation.9.clone.1 | convolution fusion | flops 203685376 | bytes 4852272 | tf_op jit(solution)/shard_map/while/body/eval_jaxpr/bhid,bwhkd->bhiwk/dot_general | solution.py:62
  151.1 2.0 gather_fusion
  153.7 3.4 %gather_fusion.3 = bf16[48,128,128]{2,1,0:T(8,128)(2,1)} fusion(bf16[32,128,128]{2,1,0:T(8,128)(2,1)} %bitcast.123, s32[1024]{0:T(1024)S(1)} %pad_clamp_fusion.6), kind=kCustom, calls=%fused_computation.3.clone.1 | custom fusion | bytes 3145920 | tf_op jit(solution)/shard_map/while/body/eval_jaxpr/gather | solution.py:60
  157.1 3.2 %fusion.70 = bf16[8,4,128,1,128]{4,2,1,3,0:T(8,128)(2,1)} fusion(bf16[8,4,128,1,128]{4,2,1,3,0:T(8,128)(2,1)} %get-tuple-element.208, s32[]{:T(128)} %get-tuple-element.207, f32[4,128,128]{2,1,0:T(8,128)S(1)} %convolution_bitcast_fusion.2, bf16[4,12,128,128]{3,2,1,0:T(8,128)(2,1)} %bitcast.124, f32[4,128,12,128]{1,3,2,0:T(8,128)S(1)} %copy-done.2, ...), kind=kOutput, calls=%fused_computation.24.clone.1 | convolution fusion | flops 205455360 | bytes 5116464 | tf_op jit(solution)/shard_map/while/body/eval_jaxpr/bhiwk,bwhkd->bhid/dot_general | solution.py:77
  160.5 2.1 gather_fusion.2
  162.7 3.1 %fusion.67 = (f32[4,128]{1,0:T(4,128)S(1)}, f32[4,128,12,128]{1,3,2,0:T(8,128)}) fusion(pred[4,12]{1,0:T(4,128)(4,1)S(1)} %iota_compare_fusion.2, bf16[4,12,128,128]{3,2,1,0:T(8,128)(2,1)S(1)} %bitcast.120, bf16[8,4,1,128,128]{3,4,1,0,2:T(8,128)(2,1)} %get-tuple-element.220, s32[]{:T(128)} %get-tuple-element.207), kind=kOutput, calls=%fused_computation.9.clone.1 | convolution fusion | flops 203685376 | bytes 4852272 | tf_op jit(solution)/shard_map/while/body/eval_jaxpr/bhid,bwhkd->bhiwk/dot_general | solution.py:62
  171.1 2.0 gather_fusion
  173.7 3.4 %gather_fusion.3 = bf16[48,128,128]{2,1,0:T(8,128)(2,1)} fusion(bf16[32,128,128]{2,1,0:T(8,128)(2,1)} %bitcast.123, s32[1024]{0:T(1024)S(1)} %pad_clamp_fusion.6), kind=kCustom, calls=%fused_computation.3.clone.1 | custom fusion | bytes 3145920 | tf_op jit(solution)/shard_map/while/body/eval_jaxpr/gather | solution.py:60
  177.2 3.2 %fusion.70 = bf16[8,4,128,1,128]{4,2,1,3,0:T(8,128)(2,1)} fusion(bf16[8,4,128,1,128]{4,2,1,3,0:T(8,128)(2,1)} %get-tuple-element.208, s32[]{:T(128)} %get-tuple-element.207, f32[4,128,128]{2,1,0:T(8,128)S(1)} %convolution_bitcast_fusion.2, bf16[4,12,128,128]{3,2,1,0:T(8,128)(2,1)} %bitcast.124, f32[4,128,12,128]{1,3,2,0:T(8,128)S(1)} %copy-done.2, ...), kind=kOutput, calls=%fused_computation.24.clone.1 | convolution fusion | flops 205455360 | bytes 5116464 | tf_op jit(solution)/shard_map/while/body/eval_jaxpr/bhiwk,bwhkd->bhid/dot_general | solution.py:77
  180.5 2.1 gather_fusion.2
  182.7 3.1 %fusion.67 = (f32[4,128]{1,0:T(4,128)S(1)}, f32[4,128,12,128]{1,3,2,0:T(8,128)}) fusion(pred[4,12]{1,0:T(4,128)(4,1)S(1)} %iota_compare_fusion.2, bf16[4,12,128,128]{3,2,1,0:T(8,128)(2,1)S(1)} %bitcast.120, bf16[8,4,1,128,128]{3,4,1,0,2:T(8,128)(2,1)} %get-tuple-element.220, s32[]{:T(128)} %get-tuple-element.207), kind=kOutput, calls=%fused_computation.9.clone.1 | convolution fusion | flops 203685376 | bytes 4852272 | tf_op jit(solution)/shard_map/while/body/eval_jaxpr/bhid,bwhkd->bhiwk/dot_general | solution.py:62
  191.2 2.0 gather_fusion
  193.8 3.4 %gather_fusion.3 = bf16[48,128,128]{2,1,0:T(8,128)(2,1)} fusion(bf16[32,128,128]{2,1,0:T(8,128)(2,1)} %bitcast.123, s32[1024]{0:T(1024)S(1)} %pad_clamp_fusion.6), kind=kCustom, calls=%fused_computation.3.clone.1 | custom fusion | bytes 3145920 | tf_op jit(solution)/shard_map/while/body/eval_jaxpr/gather | solution.py:60
  197.2 3.2 %fusion.70 = bf16[8,4,128,1,128]{4,2,1,3,0:T(8,128)(2,1)} fusion(bf16[8,4,128,1,128]{4,2,1,3,0:T(8,128)(2,1)} %get-tuple-element.208, s32[]{:T(128)} %get-tuple-element.207, f32[4,128,128]{2,1,0:T(8,128)S(1)} %convolution_bitcast_fusion.2, bf16[4,12,128,128]{3,2,1,0:T(8,128)(2,1)} %bitcast.124, f32[4,128,12,128]{1,3,2,0:T(8,128)S(1)} %copy-done.2, ...), kind=kOutput, calls=%fused_computation.24.clone.1 | convolution fusion | flops 205455360 | bytes 5116464 | tf_op jit(solution)/shard_map/while/body/eval_jaxpr/bhiwk,bwhkd->bhid/dot_general | solution.py:77
  200.5 2.1 gather_fusion.2
  202.7 3.1 %fusion.67 = (f32[4,128]{1,0:T(4,128)S(1)}, f32[4,128,12,128]{1,3,2,0:T(8,128)}) fusion(pred[4,12]{1,0:T(4,128)(4,1)S(1)} %iota_compare_fusion.2, bf16[4,12,128,128]{3,2,1,0:T(8,128)(2,1)S(1)} %bitcast.120, bf16[8,4,1,128,128]{3,4,1,0,2:T(8,128)(2,1)} %get-tuple-element.220, s32[]{:T(128)} %get-tuple-element.207), kind=kOutput, calls=%fused_computation.9.clone.1 | convolution fusion | flops 203685376 | bytes 4852272 | tf_op jit(solution)/shard_map/while/body/eval_jaxpr/bhid,bwhkd->bhiwk/dot_general | solution.py:62
  211.2 2.0 gather_fusion
  213.8 3.4 %gather_fusion.3 = bf16[48,128,128]{2,1,0:T(8,128)(2,1)} fusion(bf16[32,128,128]{2,1,0:T(8,128)(2,1)} %bitcast.123, s32[1024]{0:T(1024)S(1)} %pad_clamp_fusion.6), kind=kCustom, calls=%fused_computation.3.clone.1 | custom fusion | bytes 3145920 | tf_op jit(solution)/shard_map/while/body/eval_jaxpr/gather | solution.py:60
  217.2 3.2 %fusion.70 = bf16[8,4,128,1,128]{4,2,1,3,0:T(8,128)(2,1)} fusion(bf16[8,4,128,1,128]{4,2,1,3,0:T(8,128)(2,1)} %get-tuple-element.208, s32[]{:T(128)} %get-tuple-element.207, f32[4,128,128]{2,1,0:T(8,128)S(1)} %convolution_bitcast_fusion.2, bf16[4,12,128,128]{3,2,1,0:T(8,128)(2,1)} %bitcast.124, f32[4,128,12,128]{1,3,2,0:T(8,128)S(1)} %copy-done.2, ...), kind=kOutput, calls=%fused_computation.24.clone.1 | convolution fusion | flops 205455360 | bytes 5116464 | tf_op jit(solution)/shard_map/while/body/eval_jaxpr/bhiwk,bwhkd->bhid/dot_general | solution.py:77
  220.5 2.1 gather_fusion.2
  222.7 3.1 %fusion.67 = (f32[4,128]{1,0:T(4,128)S(1)}, f32[4,128,12,128]{1,3,2,0:T(8,128)}) fusion(pred[4,12]{1,0:T(4,128)(4,1)S(1)} %iota_compare_fusion.2, bf16[4,12,128,128]{3,2,1,0:T(8,128)(2,1)S(1)} %bitcast.120, bf16[8,4,1,128,128]{3,4,1,0,2:T(8,128)(2,1)} %get-tuple-element.220, s32[]{:T(128)} %get-tuple-element.207), kind=kOutput, calls=%fused_computation.9.clone.1 | convolution fusion | flops 203685376 | bytes 4852272 | tf_op jit(solution)/shard_map/while/body/eval_jaxpr/bhid,bwhkd->bhiwk/dot_general | solution.py:62
  231.2 2.0 gather_fusion
  233.8 3.4 %gather_fusion.3 = bf16[48,128,128]{2,1,0:T(8,128)(2,1)} fusion(bf16[32,128,128]{2,1,0:T(8,128)(2,1)} %bitcast.123, s32[1024]{0:T(1024)S(1)} %pad_clamp_fusion.6), kind=kCustom, calls=%fused_computation.3.clone.1 | custom fusion | bytes 3145920 | tf_op jit(solution)/shard_map/while/body/eval_jaxpr/gather | solution.py:60
  237.2 3.2 %fusion.70 = bf16[8,4,128,1,128]{4,2,1,3,0:T(8,128)(2,1)} fusion(bf16[8,4,128,1,128]{4,2,1,3,0:T(8,128)(2,1)} %get-tuple-element.208, s32[]{:T(128)} %get-tuple-element.207, f32[4,128,128]{2,1,0:T(8,128)S(1)} %convolution_bitcast_fusion.2, bf16[4,12,128,128]{3,2,1,0:T(8,128)(2,1)} %bitcast.124, f32[4,128,12,128]{1,3,2,0:T(8,128)S(1)} %copy-done.2, ...), kind=kOutput, calls=%fused_computation.24.clone.1 | convolution fusion | flops 205455360 | bytes 5116464 | tf_op jit(solution)/shard_map/while/body/eval_jaxpr/bhiwk,bwhkd->bhid/dot_general | solution.py:77
  240.5 2.1 gather_fusion.2
  242.7 3.1 %fusion.67 = (f32[4,128]{1,0:T(4,128)S(1)}, f32[4,128,12,128]{1,3,2,0:T(8,128)}) fusion(pred[4,12]{1,0:T(4,128)(4,1)S(1)} %iota_compare_fusion.2, bf16[4,12,128,128]{3,2,1,0:T(8,128)(2,1)S(1)} %bitcast.120, bf16[8,4,1,128,128]{3,4,1,0,2:T(8,128)(2,1)} %get-tuple-element.220, s32[]{:T(128)} %get-tuple-element.207), kind=kOutput, calls=%fused_computation.9.clone.1 | convolution fusion | flops 203685376 | bytes 4852272 | tf_op jit(solution)/shard_map/while/body/eval_jaxpr/bhid,bwhkd->bhiwk/dot_general | solution.py:62
  253.8 3.4 %gather_fusion.3 = bf16[48,128,128]{2,1,0:T(8,128)(2,1)} fusion(bf16[32,128,128]{2,1,0:T(8,128)(2,1)} %bitcast.123, s32[1024]{0:T(1024)S(1)} %pad_clamp_fusion.6), kind=kCustom, calls=%fused_computation.3.clone.1 | custom fusion | bytes 3145920 | tf_op jit(solution)/shard_map/while/body/eval_jaxpr/gather | solution.py:60
  257.2 3.2 %fusion.70 = bf16[8,4,128,1,128]{4,2,1,3,0:T(8,128)(2,1)} fusion(bf16[8,4,128,1,128]{4,2,1,3,0:T(8,128)(2,1)} %get-tuple-element.208, s32[]{:T(128)} %get-tuple-element.207, f32[4,128,128]{2,1,0:T(8,128)S(1)} %convolution_bitcast_fusion.2, bf16[4,12,128,128]{3,2,1,0:T(8,128)(2,1)} %bitcast.124, f32[4,128,12,128]{1,3,2,0:T(8,128)S(1)} %copy-done.2, ...), kind=kOutput, calls=%fused_computation.24.clone.1 | convolution fusion | flops 205455360 | bytes 5116464 | tf_op jit(solution)/shard_map/while/body/eval_jaxpr/bhiwk,bwhkd->bhid/dot_general | solution.py:77
  261.0 2.7 reduce.8
  264.0 34.9 %all_to_all.27 = bf16[32,2,8192]{2,1,0:T(2,128)(2,1)S(1)} all-to-all(bf16[32,2,8192]{2,1,0:T(2,128)(2,1)S(1)} %reshape.276), channel_id=1, replica_groups=mesh['seq'=32,'blk'=8] {'seq'}, dimensions={0} | all-to-all | bytes 2097152 | tf_op jit(solution)/shard_map/all_to_all | solution.py:96
  (185 shorter events, 62.8 us)
Async XLA Ops:
  6.5 19.4 %copy-start = (s32[256]{0:T(256)S(1)}, s32[256]{0:T(256)}, u32[]{:S(2)}) copy-start(s32[256]{0:T(256)} %param.11) | copy-start | bytes 3076
  11.9 11.8 %copy-start.4 = (bf16[4,2,128,128]{3,2,1,0:T(8,128)(2,1)S(1)}, bf16[4,2,128,128]{3,2,1,0:T(8,128)(2,1)}, u32[]{:S(2)}) copy-start(bf16[4,2,128,128]{3,2,1,0:T(8,128)(2,1)} %param.8) | copy-start | bytes 786436
  11.9 12.6 %copy-start.6 = (s32[256,8]{0,1:T(8,128)S(1)}, s32[256,8]{0,1:T(8,128)}, u32[]{:S(2)}) copy-start(s32[256,8]{0,1:T(8,128)} %param.9) | copy-start | bytes 24580
  11.9 12.7 %copy-start.5 = (s32[256,12]{0,1:T(8,128)S(1)}, s32[256,12]{0,1:T(8,128)}, u32[]{:S(2)}) copy-start(s32[256,12]{0,1:T(8,128)} %param.10) | copy-start | bytes 36868
  11.9 83.0 %all-to-all-start = ((bf16[128,3,32,128]{0,3,1,2:T(8,128)(2,1)}), bf16[128,3,32,128]{0,3,1,2:T(8,128)(2,1)S(1)}, u32[]{:S(2)}, u32[]{:S(2)}) async-start(bf16[128,3,32,128]{0,3,1,2:T(8,128)(2,1)} %copy.46), calls=%async_computation | async-start | bytes 6291456 | tf_op jit(solution)/shard_map/all_to_all | solution.py:23
  23.7 31.7 %all-gather.2.cloned.1.call-start = ((), (), s32[]{:S(2)}) async-start(), calls=%async_computation.2 | async-start | bytes 2359296 | tf_op jit(solution)/shard_map/all_gather | solution.py:31
  96.7 2.3 copy-start.3
  107.8 2.0 copy-start.1
  113.7 3.4 %copy-start.2 = (f32[4,128,12,128]{1,3,2,0:T(8,128)S(1)}, f32[4,128,12,128]{1,3,2,0:T(8,128)}, u32[]{:S(2)}) copy-start(f32[4,128,12,128]{1,3,2,0:T(8,128)} %get-tuple-element.195) | copy-start | bytes 9437188 | tf_op jit(solution)/shard_map/while
  127.8 2.0 copy-start.1
  133.7 3.4 %copy-start.2 = (f32[4,128,12,128]{1,3,2,0:T(8,128)S(1)}, f32[4,128,12,128]{1,3,2,0:T(8,128)}, u32[]{:S(2)}) copy-start(f32[4,128,12,128]{1,3,2,0:T(8,128)} %get-tuple-element.195) | copy-start | bytes 9437188 | tf_op jit(solution)/shard_map/while
  147.8 2.0 copy-start.1
  153.7 3.4 %copy-start.2 = (f32[4,128,12,128]{1,3,2,0:T(8,128)S(1)}, f32[4,128,12,128]{1,3,2,0:T(8,128)}, u32[]{:S(2)}) copy-start(f32[4,128,12,128]{1,3,2,0:T(8,128)} %get-tuple-element.195) | copy-start | bytes 9437188 | tf_op jit(solution)/shard_map/while
  167.9 2.0 copy-start.1
  173.7 3.4 %copy-start.2 = (f32[4,128,12,128]{1,3,2,0:T(8,128)S(1)}, f32[4,128,12,128]{1,3,2,0:T(8,128)}, u32[]{:S(2)}) copy-start(f32[4,128,12,128]{1,3,2,0:T(8,128)} %get-tuple-element.195) | copy-start | bytes 9437188 | tf_op jit(solution)/shard_map/while
  187.9 2.0 copy-start.1
  193.8 3.4 %copy-start.2 = (f32[4,128,12,128]{1,3,2,0:T(8,128)S(1)}, f32[4,128,12,128]{1,3,2,0:T(8,128)}, u32[]{:S(2)}) copy-start(f32[4,128,12,128]{1,3,2,0:T(8,128)} %get-tuple-element.195) | copy-start | bytes 9437188 | tf_op jit(solution)/shard_map/while
  207.9 2.0 copy-start.1
  213.8 3.4 %copy-start.2 = (f32[4,128,12,128]{1,3,2,0:T(8,128)S(1)}, f32[4,128,12,128]{1,3,2,0:T(8,128)}, u32[]{:S(2)}) copy-start(f32[4,128,12,128]{1,3,2,0:T(8,128)} %get-tuple-element.195) | copy-start | bytes 9437188 | tf_op jit(solution)/shard_map/while
  227.9 2.0 copy-start.1
  233.8 3.4 %copy-start.2 = (f32[4,128,12,128]{1,3,2,0:T(8,128)S(1)}, f32[4,128,12,128]{1,3,2,0:T(8,128)}, u32[]{:S(2)}) copy-start(f32[4,128,12,128]{1,3,2,0:T(8,128)} %get-tuple-element.195) | copy-start | bytes 9437188 | tf_op jit(solution)/shard_map/while
  247.9 2.0 copy-start.1
  253.8 3.4 %copy-start.2 = (f32[4,128,12,128]{1,3,2,0:T(8,128)S(1)}, f32[4,128,12,128]{1,3,2,0:T(8,128)}, u32[]{:S(2)}) copy-start(f32[4,128,12,128]{1,3,2,0:T(8,128)} %get-tuple-element.195) | copy-start | bytes 9437188 | tf_op jit(solution)/shard_map/while
Sparse Core Ops, SparseCore 0:
  26.3 28.9 all-gather.1
where the time goes:
time: 311 us; the launch traced here: 309 us
  local copies, waits for them, and re-layouts  101 us (32%)
  matrix products  67.9 us (22%)
  waiting for transfers between devices  65.1 us (21%)
  blocking collectives  34.9 us (11%)
  other arithmetic  13.9 us (4%)
  between operations  13.5 us (4%)
  starting transfers between devices  11.8 us (4%)
    all_to_all x1, waiting for transfers between devices, per_device(): lax.all_to_all(shaped, 'seq', split_axis=2, concat_axis=0, tiled=True)  36.5 us
    all_to_all x1, blocking collectives, per_device(): lax.all_to_all(attended, 'seq', split_axis=0, concat_axis=1, tiled=True)  34.9 us
    all_gather x1, waiting for transfers between devices, per_device(): kept_all = lax.all_gather(kept_kv, 'blk', axis=0, tiled=True)  28.6 us
    gather x8, local copies, waits for them, and re-layouts, attend(): far_values = far_values_all[kept_sel]  27.3 us
    dot_general x8, matrix products, attend(): jnp.einsum('bhiwk,bwhkd->bhid', far_weights.astype(jnp.bfloat16), far_val...  25.9 us
    dot_general x8, matrix products, attend(): jnp.einsum('bhid,bwhkd->bhiwk', queries, far_keys, preferred_element_type...  25.1 us
    gather x8, local copies, waits for them, and re-layouts, attend(): far_keys = far_keys_all[kept_sel]  16.6 us
    gather x8, local copies, waits for them, and re-layouts, attend(): near_values = near_values_all[cur_sel]  15.8 us
  transfers between devices with their start and end apart: 2, of which 2 were waited for; matrix products, arithmetic and copies ran while one was open for 2% of the time, Pallas kernels for 0%

commit v1 on v0

v1 whole, which is shorter than its diff:
```python
import functools
import math

import jax
import jax.numpy as jnp
from jax import lax
from jax.experimental import pallas as pl
from jax.experimental.pallas import tpu as pltpu
from jax.sharding import PartitionSpec as P

HEAD_DIM = 128
MASKED_SCORE = -1e30
MESH = pl.DeviceIdType.MESH
LOG2_E = 1.4426950408889634


def kernel(
    seq_count,
    blk_count,
    cur_ref,
    kept_list_ref,
    count_ref,
    qkv_ref,
    kept_ref,
    out_ref,
    stage,
    q_all,
    k_all,
    v_all,
    kept_all,
    scores,
    weights,
    partial,
    totals,
    mixed,
    stage_sem,
    kept_send,
    kept_recv,
    k_send,
    k_recv,
    q_send,
    q_recv,
    v_send,
    v_recv,
    o_send,
    o_recv,
):
    me = lax.axis_index("seq")
    region = lax.axis_index("blk")
    near_count = cur_ref.shape[0]
    window = kept_list_ref.shape[0]
    kept_own = kept_ref.shape[0]
    width = HEAD_DIM
    factor = LOG2_E / math.sqrt(width)

    order = (1, 0, 2)

    def stage_copy(slot, group, head):
        column = pl.multiple_of((group * seq_count + head) * width, width)
        return pltpu.make_async_copy(
            qkv_ref.at[:, pl.ds(column, width)], stage.at[slot, head], stage_sem.at[slot]
        )

    for slot, group in enumerate(order):

        @pl.loop(0, seq_count)
        def _(head, slot=slot, group=group):
            stage_copy(slot, group, head).start()

    barrier = pltpu.get_barrier_semaphore()

    @pl.loop(1, seq_count)
    def _(step):
        pl.semaphore_signal(
            barrier, inc=1, device_id={"seq": lax.rem(me + step, seq_count)}, device_id_type=MESH
        )

    @pl.loop(1, blk_count)
    def _(step):
        pl.semaphore_signal(
            barrier, inc=1, device_id={"blk": lax.rem(region + step, blk_count)}, device_id_type=MESH
        )

    pl.semaphore_wait(barrier, seq_count - 1 + blk_count - 1)

    buffers = (k_all, q_all, v_all)
    sends = (k_send, q_send, v_send)
    recvs = (k_recv, q_recv, v_recv)

    def send_group(slot):
        pltpu.make_async_copy(stage.at[slot], stage.at[slot], stage_sem.at[slot]).wait()
        target, send, recv = buffers[slot], sends[slot], recvs[slot]
        recv_mine = recv.at[me] if slot == 1 else recv
        pltpu.make_async_copy(stage.at[slot, me], target.at[me], recv_mine).start()

        @pl.loop(1, seq_count)
        def _(step):
            other = lax.rem(me + step, seq_count)
            pltpu.make_async_remote_copy(
                src_ref=stage.at[slot, other],
                dst_ref=target.at[me],
                send_sem=send,
                recv_sem=recv_mine,
                device_id={"seq": other},
                device_id_type=MESH,
            ).start()

    send_group(0)
    kept_mine = pl.ds(region * kept_own, kept_own)
    pltpu.make_async_copy(kept_ref, kept_all.at[kept_mine], kept_recv).start()

    @pl.loop(1, blk_count)
    def _(step):
        other = lax.rem(region + step, blk_count)
        pltpu.make_async_remote_copy(
            src_ref=kept_ref,
            dst_ref=kept_all.at[kept_mine],
            send_sem=kept_send,
            recv_sem=kept_recv,
            device_id={"blk": other},
            device_id_type=MESH,
        ).start()

    send_group(1)
    send_group(2)

    pltpu.make_async_copy(k_all, k_all, k_recv).wait()
    pltpu.make_async_copy(kept_all, kept_all, kept_recv).wait()

    contract_last = (((1,), (1,)), ((), ()))

    @pl.loop(0, seq_count)
    def _(step):
        tile = lax.rem(me + seq_count - step, seq_count)
        pltpu.make_async_copy(q_all.at[tile], q_all.at[tile], q_recv.at[tile]).wait()
        row = tile * blk_count + region
        queries = q_all[tile]
        live = count_ref[row]
        top = None
        for pair in range((near_count + window) // 2):
            first = 2 * pair
            if first < near_count:
                ids = [cur_ref[first + n, row] // blk_count for n in range(2)]
                keys = [k_all[i] for i in ids]
            else:
                slots = [first - near_count + n for n in range(2)]
                keys = [kept_all[kept_list_ref[w, row], 0] for w in slots]
            product = lax.dot_general(
                queries,
                jnp.concatenate(keys, axis=0),
                contract_last,
                preferred_element_type=jnp.float32,
            )
            for n in range(2):
                part = product[:, n * width : (n + 1) * width]
                if first >= near_count + 1 or (first >= near_count and n > 0):
                    part = part + jnp.where(first - near_count + n < live, 0.0, MASKED_SCORE)
                scores[:, pl.ds((first + n) * width, width)] = part
                top = part if top is None else jnp.maximum(top, part)
        row_max = jnp.max(top, axis=1, keepdims=True)
        total = None
        mixture = None
        for pair in range((near_count + window) // 2):
            first = 2 * pair
            weight = jnp.exp2((scores[:, pl.ds(first * width, 2 * width)] - row_max) * factor)
            half = weight[:, :width] + weight[:, width:]
            total = half if total is None else total + half
            rounded = weight.astype(jnp.bfloat16)
            if first < near_count:
                weights[tile, :, pl.ds(first * width, 2 * width)] = rounded
            else:
                slots = [first - near_count + n for n in range(2)]
                values = [kept_all[kept_list_ref[w, row], 1] for w in slots]
                term = jnp.dot(
                    rounded, jnp.concatenate(values, axis=0), preferred_element_type=jnp.float32
                )
                mixture = term if mixture is None else mixture + term
        totals[tile] = jnp.broadcast_to(jnp.sum(total, axis=1, keepdims=True), totals.shape[1:])
        partial[tile] = mixture

    pltpu.make_async_copy(v_all, v_all, v_recv).wait()

    columns_mine = pl.ds(pl.multiple_of(me * width, width), width)

    def send_out(tile):
        pltpu.make_async_remote_copy(
            src_ref=mixed.at[tile],
            dst_ref=out_ref.at[:, columns_mine],
            send_sem=o_send,
            recv_sem=o_recv,
            device_id={"seq": tile},
            device_id_type=MESH,
        ).start()

    @pl.loop(1, seq_count + 1)
    def _(step):
        tile = lax.rem(me + step, seq_count)
        row = tile * blk_count + region
        mixture = partial[tile]
        for pair in range(near_count // 2):
            first = 2 * pair
            values = [v_all[cur_ref[first + n, row] // blk_count] for n in range(2)]
            mixture = mixture + jnp.dot(
                weights[tile, :, pl.ds(first * width, 2 * width)],
                jnp.concatenate(values, axis=0),
                preferred_element_type=jnp.float32,
            )
        mixed[tile] = (mixture / totals[tile]).astype(jnp.bfloat16)

        @pl.when(step > 1)
        def _():
            send_out(lax.rem(me + step - 1, seq_count))

    own_copy = pltpu.make_async_copy(mixed.at[me], out_ref.at[:, columns_mine], o_recv)
    own_copy.start()

    others = pl.ds(0, seq_count - 1)
    for send in sends + (o_send,):
        pltpu.make_async_copy(k_all.at[others], k_all.at[others], send).wait()
    kept_others = pl.ds(0, kept_own * (blk_count - 1))
    pltpu.make_async_copy(kept_all.at[kept_others], kept_all.at[kept_others], kept_send).wait()
    pltpu.make_async_copy(out_ref, out_ref, o_recv).wait()


def per_device(qkv, kept_kv, cur_list, kept_list, kept_count):
    seq_count = lax.axis_size("seq")
    blk_count = lax.axis_size("blk")
    tile_len = qkv.shape[0]
    width = HEAD_DIM
    near_count = cur_list.shape[1]
    window = kept_list.shape[1]
    block = (tile_len, width)
    smem = pl.BlockSpec(memory_space=pltpu.SMEM)
    hbm = pl.BlockSpec(memory_space=pl.ANY)
    dma = pltpu.SemaphoreType.DMA
    return pl.pallas_call(
        functools.partial(kernel, seq_count, blk_count),
        out_shape=jax.ShapeDtypeStruct((tile_len, seq_count * width), jnp.bfloat16),
        in_specs=[smem, smem, smem, hbm, hbm],
        out_specs=pl.BlockSpec(memory_space=pltpu.VMEM),
        scratch_shapes=[
            pltpu.VMEM((3, seq_count) + block, jnp.bfloat16),
            pltpu.VMEM((seq_count,) + block, jnp.bfloat16),
            pltpu.VMEM((seq_count,) + block, jnp.bfloat16),
            pltpu.VMEM((seq_count,) + block, jnp.bfloat16),
            pltpu.VMEM((kept_kv.shape[0] * blk_count, 2) + block, jnp.bfloat16),
            pltpu.VMEM((tile_len, (near_count + window) * width), jnp.float32),
            pltpu.VMEM((seq_count, tile_len, near_count * width), jnp.bfloat16),
            pltpu.VMEM((seq_count,) + block, jnp.float32),
            pltpu.VMEM((seq_count,) + block, jnp.float32),
            pltpu.VMEM((seq_count,) + block, jnp.bfloat16),
            dma((3,)),
            dma,
            dma,
            dma,
            dma,
            dma,
            dma((seq_count,)),
            dma,
            dma,
            dma,
            dma,
        ],
        compiler_params=pltpu.CompilerParams(
            collective_id=0, has_side_effects=True, vmem_limit_bytes=50 << 20
        ),
    )(cur_list.T, kept_list.T, kept_count, qkv, kept_kv)


def solution(mesh):
    placed = (P(("seq", "blk"), None), P("blk", None, None, "seq"), P(), P(), P())
    return jax.shard_map(
        per_device, mesh=mesh, in_specs=placed, out_specs=P(("seq", "blk"), None), check_vma=False
    )
```

time: 311 us -> 114 us (0.37)
  Pallas kernels: 0 us -> 109 us
  local copies, waits for them, and re-layouts: 101 us -> 4.01 us
  matrix products: 67.9 us -> 0 us
  waiting for transfers between devices: 65.1 us -> 0 us
  blocking collectives: 34.9 us -> 0 us
  other arithmetic: 13.9 us -> 0 us
  between operations: 13.5 us -> 0.01 us
  starting transfers between devices: 11.8 us -> 0 us
    pallas_call x0 -> x1, Pallas kernels: none -> 109 us  [per_device(): pl.pallas_call(functools.partial(kernel, seq_count, blk_count), out_shape...]
    gather x35 -> x0, local copies, waits for them, and re-layouts: 77.3 us -> none  [the longest x8 27.3 us: attend(): far_values = far_values_all[kept_sel]]
    dot_general x32 -> x0, matrix products: 67.9 us -> none  [the longest x8 25.9 us: attend(): jnp.einsum('bhiwk,bwhkd->bhid', far_weights.astype(jnp.bfloat16), far_val...]
    all_to_all x1 -> x0, waiting for transfers between devices: 36.5 us -> none  [per_device(): lax.all_to_all(shaped, 'seq', split_axis=2, concat_axis=0, tiled=True)]
    all_to_all x1 -> x0, blocking collectives: 34.9 us -> none  [per_device(): lax.all_to_all(attended, 'seq', split_axis=0, concat_axis=1, tiled=True)]
    all_gather x1 -> x0, waiting for transfers between devices: 28.6 us -> none  [per_device(): kept_all = lax.all_gather(kept_kv, 'blk', axis=0, tiled=True)]
    all_to_all x1 -> x0, starting transfers between devices: 11.7 us -> none  [per_device(): lax.all_to_all(shaped, 'seq', split_axis=2, concat_axis=0, tiled=True)]
    reduce_sum x16 -> x0, other arithmetic: 10.4 us -> none  [attend(): row_total = near_weights.sum(axis=(3, 4)) + far_weights.sum(axis=(3, 4))]
  transfers between devices with their start and end apart: 2 -> 0, of which waited for: 2 -> 0; matrix products, arithmetic and copies ran while one was open for 2% -> 0% of each run, Pallas kernels for 0% -> 0%
where the time goes in v1:
time: 114 us; the launch traced here: 113 us
  Pallas kernels  109 us (96%)
  local copies, waits for them, and re-layouts  4.01 us (4%)
    pallas_call x1, Pallas kernels, per_device(): pl.pallas_call(functools.partial(kernel, seq_count, blk_count), out_shape...  109 us
    unnamed x9, local copies, waits for them, and re-layouts  4.01 us

profile of v1, /device:TPU:2, one launch (start us, length us, event | category | flops | bytes accessed | tf_op | source)
XLA Modules:
  0.0 113.4 jit_solution(9751493359741816407)
XLA Ops:
  0.0 0.0 copy-start
  0.0 0.9 copy-done
  1.0 0.0 copy-start.1
  1.0 0.7 copy-done.1
  1.7 0.0 copy-start.2
  1.7 0.7 copy-done.2
  2.4 0.0 copy-start.3
  2.4 0.7 copy-done.3
  3.0 109.4 %shard_map.55 = bf16[128,4096]{1,0:T(8,128)(2,1)S(1)} custom-call(s32[8,256]{1,0:T(8,128)S(1)} %bitcast.3, s32[12,256]{1,0:T(8,128)S(1)} %bitcast.2, s32[256]{0:T(256)S(1)} %copy-done.3, bf16[128,12288]{1,0:T(8,128)(2,1)} %qkv_ref.1, bf16[4,2,128,128]{3,2,1,0:T(8,128)(2,1)S(1)} %copy-done), custom_call_target="tpu_custom_call" | custom-call | tf_op jit(solution)/shard_map/pallas_call | solution.py:236
  112.5 1.0 copy.7
Async XLA Ops:
  0.0 0.9 copy-start
  1.0 0.7 copy-start.1
  1.7 0.7 copy-start.2
  2.4 0.7 copy-start.3

commit v2 on v1

--- a/solution.py
+++ b/solution.py
@@ -17,22 +17,23 @@
 def kernel(
     seq_count,
     blk_count,
+    cur_hbm,
+    kept_list_hbm,
+    count_hbm,
+    qkv_ref,
+    kept_ref,
+    out_ref,
     cur_ref,
     kept_list_ref,
     count_ref,
-    qkv_ref,
-    kept_ref,
-    out_ref,
     stage,
     q_all,
     k_all,
     v_all,
     kept_all,
     scores,
-    weights,
-    partial,
-    totals,
     mixed,
+    list_sem,
     stage_sem,
     kept_send,
     kept_recv,
@@ -53,7 +54,7 @@
     width = HEAD_DIM
     factor = LOG2_E / math.sqrt(width)
 
-    order = (1, 0, 2)
+    order = (1, 2, 0)
 
     def stage_copy(slot, group, head):
         column = pl.multiple_of((group * seq_count + head) * width, width)
@@ -67,6 +68,14 @@
         def _(head, slot=slot, group=group):
             stage_copy(slot, group, head).start()
 
+    lists = ((cur_hbm, cur_ref), (kept_list_hbm, kept_list_ref), (count_hbm, count_ref))
+    list_copies = [
+        pltpu.make_async_copy(source, target, list_sem.at[n])
+        for n, (source, target) in enumerate(lists)
+    ]
+    for copy in list_copies:
+        copy.start()
+
     barrier = pltpu.get_barrier_semaphore()
 
     @pl.loop(1, seq_count)
@@ -83,14 +92,14 @@
 
     pl.semaphore_wait(barrier, seq_count - 1 + blk_count - 1)
 
-    buffers = (k_all, q_all, v_all)
-    sends = (k_send, q_send, v_send)
-    recvs = (k_recv, q_recv, v_recv)
+    buffers = (k_all, v_all, q_all)
+    sends = (k_send, v_send, q_send)
+    recvs = (k_recv, v_recv, q_recv)
 
     def send_group(slot):
         pltpu.make_async_copy(stage.at[slot], stage.at[slot], stage_sem.at[slot]).wait()
         target, send, recv = buffers[slot], sends[slot], recvs[slot]
-        recv_mine = recv.at[me] if slot == 1 else recv
+        recv_mine = recv.at[me] if slot == 2 else recv
         pltpu.make_async_copy(stage.at[slot, me], target.at[me], recv_mine).start()
 
         @pl.loop(1, seq_count)
@@ -124,8 +133,23 @@
     send_group(1)
     send_group(2)
 
+    for copy in list_copies:
+        copy.wait()
     pltpu.make_async_copy(k_all, k_all, k_recv).wait()
     pltpu.make_async_copy(kept_all, kept_all, kept_recv).wait()
+    pltpu.make_async_copy(v_all, v_all, v_recv).wait()
+
+    columns_mine = pl.ds(pl.multiple_of(me * width, width), width)
+
+    def send_out(tile):
+        pltpu.make_async_remote_copy(
+            src_ref=mixed.at[tile],
+            dst_ref=out_ref.at[:, columns_mine],
+            send_sem=o_send,
+            recv_sem=o_recv,
+            device_id={"seq": tile},
+            device_id_type=MESH,
+        ).start()
 
     contract_last = (((1,), (1,)), ((), ()))
 
@@ -167,50 +191,23 @@
             total = half if total is None else total + half
             rounded = weight.astype(jnp.bfloat16)
             if first < near_count:
-                weights[tile, :, pl.ds(first * width, 2 * width)] = rounded
+                ids = [cur_ref[first + n, row] // blk_count for n in range(2)]
+                values = [v_all[i] for i in ids]
             else:
                 slots = [first - near_count + n for n in range(2)]
                 values = [kept_all[kept_list_ref[w, row], 1] for w in slots]
-                term = jnp.dot(
-                    rounded, jnp.concatenate(values, axis=0), preferred_element_type=jnp.float32
-                )
-                mixture = term if mixture is None else mixture + term
-        totals[tile] = jnp.broadcast_to(jnp.sum(total, axis=1, keepdims=True), totals.shape[1:])
-        partial[tile] = mixture
-
-    pltpu.make_async_copy(v_all, v_all, v_recv).wait()
-
-    columns_mine = pl.ds(pl.multiple_of(me * width, width), width)
-
-    def send_out(tile):
-        pltpu.make_async_remote_copy(
-            src_ref=mixed.at[tile],
-            dst_ref=out_ref.at[:, columns_mine],
-            send_sem=o_send,
-            recv_sem=o_recv,
-            device_id={"seq": tile},
-            device_id_type=MESH,
-        ).start()
-
-    @pl.loop(1, seq_count + 1)
-    def _(step):
-        tile = lax.rem(me + step, seq_count)
-        row = tile * blk_count + region
-        mixture = partial[tile]
-        for pair in range(near_count // 2):
-            first = 2 * pair
-            values = [v_all[cur_ref[first + n, row] // blk_count] for n in range(2)]
-            mixture = mixture + jnp.dot(
-                weights[tile, :, pl.ds(first * width, 2 * width)],
-                jnp.concatenate(values, axis=0),
-                preferred_element_type=jnp.float32,
+            term = jnp.dot(
+                rounded, jnp.concatenate(values, axis=0), preferred_element_type=jnp.float32
             )
-        mixed[tile] = (mixture / totals[tile]).astype(jnp.bfloat16)
+            mixture = term if mixture is None else mixture + term
+        row_total = jnp.sum(total, axis=1, keepdims=True)
+        mixed[tile] = (mixture / row_total).astype(jnp.bfloat16)
 
         @pl.when(step > 1)
         def _():
-            send_out(lax.rem(me + step - 1, seq_count))
-
+            send_out(lax.rem(me + seq_count - step + 1, seq_count))
+
+    send_out(lax.rem(me + 1, seq_count))
     own_copy = pltpu.make_async_copy(mixed.at[me], out_ref.at[:, columns_mine], o_recv)
     own_copy.start()
 
@@ -230,25 +227,25 @@
     near_count = cur_list.shape[1]
     window = kept_list.shape[1]
     block = (tile_len, width)
-    smem = pl.BlockSpec(memory_space=pltpu.SMEM)
-    hbm = pl.BlockSpec(memory_space=pl.ANY)
+    hbm = pl.BlockSpec(memory_space=pltpu.HBM)
     dma = pltpu.SemaphoreType.DMA
     return pl.pallas_call(
         functools.partial(kernel, seq_count, blk_count),
         out_shape=jax.ShapeDtypeStruct((tile_len, seq_count * width), jnp.bfloat16),
-        in_specs=[smem, smem, smem, hbm, hbm],
+        in_specs=[hbm] * 5,
         out_specs=pl.BlockSpec(memory_space=pltpu.VMEM),
         scratch_shapes=[
+            pltpu.SMEM(cur_list.shape[::-1], jnp.int32),
+            pltpu.SMEM(kept_list.shape[::-1], jnp.int32),
+            pltpu.SMEM(kept_count.shape, jnp.int32),
             pltpu.VMEM((3, seq_count) + block, jnp.bfloat16),
             pltpu.VMEM((seq_count,) + block, jnp.bfloat16),
             pltpu.VMEM((seq_count,) + block, jnp.bfloat16),
             pltpu.VMEM((seq_count,) + block, jnp.bfloat16),
             pltpu.VMEM((kept_kv.shape[0] * blk_count, 2) + block, jnp.bfloat16),
             pltpu.VMEM((tile_len, (near_count + window) * width), jnp.float32),
-            pltpu.VMEM((seq_count, tile_len, near_count * width), jnp.bfloat16),
-            pltpu.VMEM((seq_count,) + block, jnp.float32),
-            pltpu.VMEM((seq_count,) + block, jnp.float32),
-            pltpu.VMEM((seq_count,) + block, jnp.bfloat16),
+            pltpu.VMEM((seq_count,) + block, jnp.bfloat16),
+            dma((3,)),
             dma((3,)),
             dma,
             dma,
@@ -264,7 +261,7 @@
         compiler_params=pltpu.CompilerParams(
             collective_id=0, has_side_effects=True, vmem_limit_bytes=50 << 20
         ),
-    )(cur_list.T, kept_list.T, kept_count, qkv, kept_kv)
+    )(*(pltpu.with_memory_space_constraint(a, pltpu.HBM) for a in (cur_list.T, kept_list.T, kept_count, qkv, kept_kv)))
 
 
 def solution(mesh):

time: 114 us -> 109 us (0.956); the launches traced: 113 us -> 107 us
  local copies, waits for them, and re-layouts: 4.01 us -> 0.97 us
  Pallas kernels: 109 us -> 106 us
    pallas_call x1, Pallas kernels: 109 us -> 106 us  [per_device(): pl.pallas_call(functools.partial(kernel, seq_count, blk_count), out_shape...]
    unnamed x9 -> x1, local copies, waits for them, and re-layouts: 4.01 us -> 0.97 us
where the time goes in v2:
time: 109 us; the launch traced here: 107 us
  Pallas kernels  106 us (97%)
    pallas_call x1, Pallas kernels, per_device(): pl.pallas_call(functools.partial(kernel, seq_count, blk_count), out_shape...  106 us

profile of v2, /device:TPU:2, one launch (start us, length us, event | category | flops | bytes accessed | tf_op | source)
XLA Modules:
  0.0 107.2 jit_solution(12444213595836515507)
XLA Ops:
  0.0 106.3 %shard_map.55 = bf16[128,4096]{1,0:T(8,128)(2,1)S(1)} custom-call(s32[8,256]{1,0:T(8,128)} %bitcast.3, s32[12,256]{1,0:T(8,128)} %bitcast.2, s32[256]{0:T(256)} %count_hbm.1, bf16[128,12288]{1,0:T(8,128)(2,1)} %qkv_ref.1, bf16[4,2,128,128]{3,2,1,0:T(8,128)(2,1)} %kept_ref.1), custom_call_target="tpu_custom_call" | custom-call | tf_op jit(solution)/shard_map/pallas_call | solution.py:232
  106.3 1.0 copy.7

commit v3 on v2

--- a/solution.py
+++ b/solution.py
@@ -17,6 +17,7 @@
 def kernel(
     seq_count,
     blk_count,
+    rows,
     cur_hbm,
     kept_list_hbm,
     count_hbm,
@@ -47,12 +48,38 @@
     o_recv,
 ):
     me = lax.axis_index("seq")
+    rings = seq_count // rows
+    my_z = me // rows
+    my_x = lax.rem(me, rows)
+
+    def partner(step, back):
+        turn = lax.rem(step, rings)
+        far = (turn + 1) // 2 * (1 - 2 * lax.rem(turn, 2)) + rings // 2
+        side = lax.rem(step // rings + 1, rows)
+        if back:
+            far, side = rings - far, rows - side
+        return lax.rem(my_z + far, rings) * rows + lax.rem(my_x + side, rows)
+
     region = lax.axis_index("blk")
     near_count = cur_ref.shape[0]
     window = kept_list_ref.shape[0]
     kept_own = kept_ref.shape[0]
     width = HEAD_DIM
     factor = LOG2_E / math.sqrt(width)
+
+    barrier = pltpu.get_barrier_semaphore()
+
+    @pl.loop(0, seq_count - 1)
+    def _(step):
+        pl.semaphore_signal(
+            barrier, inc=1, device_id={"seq": partner(step, False)}, device_id_type=MESH
+        )
+
+    @pl.loop(1, blk_count)
+    def _(step):
+        pl.semaphore_signal(
+            barrier, inc=1, device_id={"blk": lax.rem(region + step, blk_count)}, device_id_type=MESH
+        )
 
     order = (1, 2, 0)
 
@@ -76,20 +103,6 @@
     for copy in list_copies:
         copy.start()
 
-    barrier = pltpu.get_barrier_semaphore()
-
-    @pl.loop(1, seq_count)
-    def _(step):
-        pl.semaphore_signal(
-            barrier, inc=1, device_id={"seq": lax.rem(me + step, seq_count)}, device_id_type=MESH
-        )
-
-    @pl.loop(1, blk_count)
-    def _(step):
-        pl.semaphore_signal(
-            barrier, inc=1, device_id={"blk": lax.rem(region + step, blk_count)}, device_id_type=MESH
-        )
-
     pl.semaphore_wait(barrier, seq_count - 1 + blk_count - 1)
 
     buffers = (k_all, v_all, q_all)
@@ -102,9 +115,9 @@
         recv_mine = recv.at[me] if slot == 2 else recv
         pltpu.make_async_copy(stage.at[slot, me], target.at[me], recv_mine).start()
 
-        @pl.loop(1, seq_count)
+        @pl.loop(0, seq_count - 1)
         def _(step):
-            other = lax.rem(me + step, seq_count)
+            other = partner(step, False)
             pltpu.make_async_remote_copy(
                 src_ref=stage.at[slot, other],
                 dst_ref=target.at[me],
@@ -155,7 +168,7 @@
 
     @pl.loop(0, seq_count)
     def _(step):
-        tile = lax.rem(me + seq_count - step, seq_count)
+        tile = partner(step, True)
         pltpu.make_async_copy(q_all.at[tile], q_all.at[tile], q_recv.at[tile]).wait()
         row = tile * blk_count + region
         queries = q_all[tile]
@@ -203,11 +216,10 @@
         row_total = jnp.sum(total, axis=1, keepdims=True)
         mixed[tile] = (mixture / row_total).astype(jnp.bfloat16)
 
-        @pl.when(step > 1)
+        @pl.when(step > 0)
         def _():
-            send_out(lax.rem(me + seq_count - step + 1, seq_count))
-
-    send_out(lax.rem(me + 1, seq_count))
+            send_out(partner(step - 1, True))
+
     own_copy = pltpu.make_async_copy(mixed.at[me], out_ref.at[:, columns_mine], o_recv)
     own_copy.start()
 
@@ -230,7 +242,7 @@
     hbm = pl.BlockSpec(memory_space=pltpu.HBM)
     dma = pltpu.SemaphoreType.DMA
     return pl.pallas_call(
-        functools.partial(kernel, seq_count, blk_count),
+        functools.partial(kernel, seq_count, blk_count, 4),
         out_shape=jax.ShapeDtypeStruct((tile_len, seq_count * width), jnp.bfloat16),
         in_specs=[hbm] * 5,
         out_specs=pl.BlockSpec(memory_space=pltpu.VMEM),

time: 109 us -> 103 us (0.945)
  Pallas kernels: 106 us -> 101 us
    pallas_call x1, Pallas kernels: 106 us -> 101 us  [per_device(): pl.pallas_call(functools.partial(kernel, seq_count, blk_count, 4), out_sh...]
where the time goes in v3:
time: 103 us; the launch traced here: 102 us
  Pallas kernels  101 us (98%)
    pallas_call x1, Pallas kernels, per_device(): pl.pallas_call(functools.partial(kernel, seq_count, blk_count, 4), out_sh...  101 us

profile of v3, /device:TPU:2, one launch (start us, length us, event | category | flops | bytes accessed | tf_op | source)
XLA Modules:
  0.0 102.1 jit_solution(4350649387163685060)
XLA Ops:
  0.0 101.2 %shard_map.55 = bf16[128,4096]{1,0:T(8,128)(2,1)S(1)} custom-call(s32[8,256]{1,0:T(8,128)} %bitcast.3, s32[12,256]{1,0:T(8,128)} %bitcast.2, s32[256]{0:T(256)} %count_hbm.1, bf16[128,12288]{1,0:T(8,128)(2,1)} %qkv_ref.1, bf16[4,2,128,128]{3,2,1,0:T(8,128)(2,1)} %kept_ref.1), custom_call_target="tpu_custom_call" | custom-call | tf_op jit(solution)/shard_map/pallas_call | solution.py:244
  101.2 1.0 copy.7

commit v4 on v3

--- a/solution.py
+++ b/solution.py
@@ -46,19 +46,36 @@
     v_recv,
     o_send,
     o_recv,
+    level_sem,
 ):
     me = lax.axis_index("seq")
     rings = seq_count // rows
     my_z = me // rows
     my_x = lax.rem(me, rows)
 
-    def partner(step, back):
+    z_at = [lax.rem(my_z + far, rings) for far in range(rings)]
+    x_at = [lax.rem(my_x + side, rows) for side in range(rows)]
+
+    def place(far, side):
+        return z_at[far] * rows + x_at[side]
+
+    def hops(far, side):
+        return min(far, rings - far) + min(side, rows - side)
+
+    turns = [rings // 2]
+    for far in range(rings // 2 - 1, 0, -1):
+        turns += [far, rings - far]
+    turns += [0]
+    partners = [(far, side % rows) for side in range(1, rows + 1) for far in turns]
+    partners.remove((0, 0))
+    reach = rings // 2 + rows // 2
+    neighbours = [place(far, side) for far, side in partners if hops(far, side) == 1]
+
+    def source(step):
         turn = lax.rem(step, rings)
         far = (turn + 1) // 2 * (1 - 2 * lax.rem(turn, 2)) + rings // 2
         side = lax.rem(step // rings + 1, rows)
-        if back:
-            far, side = rings - far, rows - side
-        return lax.rem(my_z + far, rings) * rows + lax.rem(my_x + side, rows)
+        return lax.rem(my_z + far, rings) * rows + lax.rem(my_x + rows - side, rows)
 
     region = lax.axis_index("blk")
     near_count = cur_ref.shape[0]
@@ -69,11 +86,8 @@
 
     barrier = pltpu.get_barrier_semaphore()
 
-    @pl.loop(0, seq_count - 1)
-    def _(step):
-        pl.semaphore_signal(
-            barrier, inc=1, device_id={"seq": partner(step, False)}, device_id_type=MESH
-        )
+    for neighbour in neighbours:
+        pl.semaphore_signal(barrier, inc=1, device_id={"seq": neighbour}, device_id_type=MESH)
 
     @pl.loop(1, blk_count)
     def _(step):
@@ -103,33 +117,48 @@
     for copy in list_copies:
         copy.start()
 
-    pl.semaphore_wait(barrier, seq_count - 1 + blk_count - 1)
+    for slot in range(3):
+        pltpu.make_async_copy(stage.at[slot], stage.at[slot], stage_sem.at[slot]).wait()
+
+    pl.semaphore_wait(barrier, len(neighbours) + blk_count - 1)
+
+    def tell(level):
+        for neighbour in neighbours:
+            pl.semaphore_signal(
+                level_sem.at[level], inc=1, device_id={"seq": neighbour}, device_id_type=MESH
+            )
+
+    tell(0)
 
     buffers = (k_all, v_all, q_all)
     sends = (k_send, v_send, q_send)
     recvs = (k_recv, v_recv, q_recv)
 
-    def send_group(slot):
-        pltpu.make_async_copy(stage.at[slot], stage.at[slot], stage_sem.at[slot]).wait()
+    def send_group(slot, nearest, farthest):
         target, send, recv = buffers[slot], sends[slot], recvs[slot]
         recv_mine = recv.at[me] if slot == 2 else recv
-        pltpu.make_async_copy(stage.at[slot, me], target.at[me], recv_mine).start()
-
-        @pl.loop(0, seq_count - 1)
-        def _(step):
-            other = partner(step, False)
-            pltpu.make_async_remote_copy(
-                src_ref=stage.at[slot, other],
-                dst_ref=target.at[me],
-                send_sem=send,
-                recv_sem=recv_mine,
-                device_id={"seq": other},
-                device_id_type=MESH,
-            ).start()
-
-    send_group(0)
+
+        for far, side in partners:
+            if nearest <= hops(far, side) <= farthest:
+                other = place(far, side)
+                pltpu.make_async_remote_copy(
+                    src_ref=stage.at[slot, other],
+                    dst_ref=target.at[me],
+                    send_sem=send,
+                    recv_sem=recv_mine,
+                    device_id={"seq": other},
+                    device_id_type=MESH,
+                ).start()
+
+    send_group(0, 1, 1)
+    send_group(1, 1, 1)
+
+    pl.semaphore_wait(level_sem.at[0], len(neighbours))
+    tell(1)
+    send_group(0, 2, 2)
+    send_group(1, 2, 2)
+
     kept_mine = pl.ds(region * kept_own, kept_own)
-    pltpu.make_async_copy(kept_ref, kept_all.at[kept_mine], kept_recv).start()
 
     @pl.loop(1, blk_count)
     def _(step):
@@ -143,8 +172,19 @@
             device_id_type=MESH,
         ).start()
 
-    send_group(1)
-    send_group(2)
+    pltpu.make_async_copy(kept_ref, kept_all.at[kept_mine], kept_recv).start()
+    for slot in range(3):
+        recv = recvs[slot].at[me] if slot == 2 else recvs[slot]
+        pltpu.make_async_copy(stage.at[slot, me], buffers[slot].at[me], recv).start()
+
+    for level in range(1, reach - 1):
+        pl.semaphore_wait(level_sem.at[level], len(neighbours))
+        if level < reach - 2:
+            tell(level + 1)
+        send_group(0, level + 2, level + 2)
+        send_group(1, level + 2, level + 2)
+
+    send_group(2, 1, reach)
 
     for copy in list_copies:
         copy.wait()
@@ -168,7 +208,7 @@
 
     @pl.loop(0, seq_count)
     def _(step):
-        tile = partner(step, True)
+        tile = source(step)
         pltpu.make_async_copy(q_all.at[tile], q_all.at[tile], q_recv.at[tile]).wait()
         row = tile * blk_count + region
         queries = q_all[tile]
@@ -218,7 +258,7 @@
 
         @pl.when(step > 0)
         def _():
-            send_out(partner(step - 1, True))
+            send_out(source(step - 1))
 
     own_copy = pltpu.make_async_copy(mixed.at[me], out_ref.at[:, columns_mine], o_recv)
     own_copy.start()
@@ -269,6 +309,7 @@
             dma,
             dma,
             dma,
+            pltpu.SemaphoreType.REGULAR((seq_count // 8 + 1,)),
         ],
         compiler_params=pltpu.CompilerParams(
             collective_id=0, has_side_effects=True, vmem_limit_bytes=50 << 20

time: 103 us -> 102 us (level)
  no operation moved by 1% of the time
where the time goes in v4:
time: 102 us; the launch traced here: 101 us
  Pallas kernels  100 us (98%)
    pallas_call x1, Pallas kernels, per_device(): pl.pallas_call(functools.partial(kernel, seq_count, blk_count, 4), out_sh...  100 us

profile of v4, /device:TPU:2, one launch (start us, length us, event | category | flops | bytes accessed | tf_op | source)
XLA Modules:
  0.0 101.3 jit_solution(1954091920456021249)
XLA Ops:
  0.0 100.4 %shard_map.55 = bf16[128,4096]{1,0:T(8,128)(2,1)S(1)} custom-call(s32[8,256]{1,0:T(8,128)} %bitcast.3, s32[12,256]{1,0:T(8,128)} %bitcast.2, s32[256]{0:T(256)} %count_hbm.1, bf16[128,12288]{1,0:T(8,128)(2,1)} %qkv_ref.1, bf16[4,2,128,128]{3,2,1,0:T(8,128)(2,1)} %kept_ref.1), custom_call_target="tpu_custom_call" | custom-call | tf_op jit(solution)/shard_map/pallas_call | solution.py:284
  100.4 1.0 copy.7

commit v5 on v4

--- a/solution.py
+++ b/solution.py
@@ -18,6 +18,7 @@
     seq_count,
     blk_count,
     rows,
+    cores,
     cur_hbm,
     kept_list_hbm,
     count_hbm,
@@ -47,6 +48,7 @@
     o_send,
     o_recv,
     level_sem,
+    blk_sem,
 ):
     me = lax.axis_index("seq")
     rings = seq_count // rows
@@ -78,6 +80,16 @@
         return lax.rem(my_z + far, rings) * rows + lax.rem(my_x + rows - side, rows)
 
     region = lax.axis_index("blk")
+    my_y = region // cores
+    my_core = lax.rem(region, cores)
+    columns = blk_count // cores
+
+    def blk_place(along, core):
+        return lax.rem(my_y + along, columns) * cores + lax.rem(my_core + core, cores)
+
+    blk_partners = [(along, core) for core in range(cores) for along in range(columns)]
+    blk_partners.remove((0, 0))
+    blk_neighbours = [blk_place(*at) for at in ((1, 0), (columns - 1, 0), (0, 1))]
     near_count = cur_ref.shape[0]
     window = kept_list_ref.shape[0]
     kept_own = kept_ref.shape[0]
@@ -89,11 +101,8 @@
     for neighbour in neighbours:
         pl.semaphore_signal(barrier, inc=1, device_id={"seq": neighbour}, device_id_type=MESH)
 
-    @pl.loop(1, blk_count)
-    def _(step):
-        pl.semaphore_signal(
-            barrier, inc=1, device_id={"blk": lax.rem(region + step, blk_count)}, device_id_type=MESH
-        )
+    for neighbour in blk_neighbours:
+        pl.semaphore_signal(barrier, inc=1, device_id={"blk": neighbour}, device_id_type=MESH)
 
     order = (1, 2, 0)
 
@@ -117,10 +126,7 @@
     for copy in list_copies:
         copy.start()
 
-    for slot in range(3):
-        pltpu.make_async_copy(stage.at[slot], stage.at[slot], stage_sem.at[slot]).wait()
-
-    pl.semaphore_wait(barrier, len(neighbours) + blk_count - 1)
+    pl.semaphore_wait(barrier, len(neighbours) + len(blk_neighbours))
 
     def tell(level):
         for neighbour in neighbours:
@@ -128,7 +134,17 @@
                 level_sem.at[level], inc=1, device_id={"seq": neighbour}, device_id_type=MESH
             )
 
+    def tell_blk(level):
+        for neighbour in blk_neighbours:
+            pl.semaphore_signal(
+                blk_sem.at[level], inc=1, device_id={"blk": neighbour}, device_id_type=MESH
+            )
+
+    def staged(slot):
+        pltpu.make_async_copy(stage.at[slot], stage.at[slot], stage_sem.at[slot]).wait()
+
     tell(0)
+    tell_blk(0)
 
     buffers = (k_all, v_all, q_all)
     sends = (k_send, v_send, q_send)
@@ -150,27 +166,20 @@
                     device_id_type=MESH,
                 ).start()
 
+    staged(0)
     send_group(0, 1, 1)
+    staged(1)
     send_group(1, 1, 1)
 
     pl.semaphore_wait(level_sem.at[0], len(neighbours))
     tell(1)
     send_group(0, 2, 2)
+    pl.semaphore_wait(blk_sem.at[0], len(blk_neighbours))
+    tell_blk(1)
     send_group(1, 2, 2)
+    staged(2)
 
     kept_mine = pl.ds(region * kept_own, kept_own)
-
-    @pl.loop(1, blk_count)
-    def _(step):
-        other = lax.rem(region + step, blk_count)
-        pltpu.make_async_remote_copy(
-            src_ref=kept_ref,
-            dst_ref=kept_all.at[kept_mine],
-            send_sem=kept_send,
-            recv_sem=kept_recv,
-            device_id={"blk": other},
-            device_id_type=MESH,
-        ).start()
 
     pltpu.make_async_copy(kept_ref, kept_all.at[kept_mine], kept_recv).start()
     for slot in range(3):
@@ -183,6 +192,17 @@
             tell(level + 1)
         send_group(0, level + 2, level + 2)
         send_group(1, level + 2, level + 2)
+
+    pl.semaphore_wait(blk_sem.at[1], len(blk_neighbours))
+    for along, core in blk_partners:
+        pltpu.make_async_remote_copy(
+            src_ref=kept_ref,
+            dst_ref=kept_all.at[kept_mine],
+            send_sem=kept_send,
+            recv_sem=kept_recv,
+            device_id={"blk": blk_place(along, core)},
+            device_id_type=MESH,
+        ).start()
 
     send_group(2, 1, reach)
 
@@ -282,7 +302,7 @@
     hbm = pl.BlockSpec(memory_space=pltpu.HBM)
     dma = pltpu.SemaphoreType.DMA
     return pl.pallas_call(
-        functools.partial(kernel, seq_count, blk_count, 4),
+        functools.partial(kernel, seq_count, blk_count, 4, 2),
         out_shape=jax.ShapeDtypeStruct((tile_len, seq_count * width), jnp.bfloat16),
         in_specs=[hbm] * 5,
         out_specs=pl.BlockSpec(memory_space=pltpu.VMEM),
@@ -310,6 +330,7 @@
             dma,
             dma,
             pltpu.SemaphoreType.REGULAR((seq_count // 8 + 1,)),
+            pltpu.SemaphoreType.REGULAR((2,)),
         ],
         compiler_params=pltpu.CompilerParams(
             collective_id=0, has_side_effects=True, vmem_limit_bytes=50 << 20

time: 102 us -> 101 us (level)
  no operation moved by 1% of the time
where the time goes in v5:
time: 101 us
  Pallas kernels  100 us (99%)
    pallas_call x1, Pallas kernels, per_device(): pl.pallas_call(functools.partial(kernel, seq_count, blk_count, 4, 2), out...  100 us

profile of v5, /device:TPU:2, one launch (start us, length us, event | category | flops | bytes accessed | tf_op | source)
XLA Modules:
  0.0 101.2 jit_solution(2579483211458623707)
XLA Ops:
  0.0 100.2 %shard_map.55 = bf16[128,4096]{1,0:T(8,128)(2,1)S(1)} custom-call(s32[8,256]{1,0:T(8,128)} %bitcast.3, s32[12,256]{1,0:T(8,128)} %bitcast.2, s32[256]{0:T(256)} %count_hbm.1, bf16[128,12288]{1,0:T(8,128)(2,1)} %qkv_ref.1, bf16[4,2,128,128]{3,2,1,0:T(8,128)(2,1)} %kept_ref.1), custom_call_target="tpu_custom_call" | custom-call | tf_op jit(solution)/shard_map/pallas_call | solution.py:304
  100.2 1.0 copy.7

commit v6 on v5

--- a/solution.py
+++ b/solution.py
@@ -28,23 +28,18 @@
     cur_ref,
     kept_list_ref,
     count_ref,
-    stage,
     q_all,
-    k_all,
-    v_all,
+    kv_all,
     kept_all,
     scores,
     mixed,
     list_sem,
-    stage_sem,
     kept_send,
     kept_recv,
-    k_send,
-    k_recv,
+    kv_send,
+    kv_recv,
     q_send,
     q_recv,
-    v_send,
-    v_recv,
     o_send,
     o_recv,
     level_sem,
@@ -73,11 +68,13 @@
     reach = rings // 2 + rows // 2
     neighbours = [place(far, side) for far, side in partners if hops(far, side) == 1]
 
-    def source(step):
+    def partner(step, back):
         turn = lax.rem(step, rings)
         far = (turn + 1) // 2 * (1 - 2 * lax.rem(turn, 2)) + rings // 2
         side = lax.rem(step // rings + 1, rows)
-        return lax.rem(my_z + far, rings) * rows + lax.rem(my_x + rows - side, rows)
+        if back:
+            far, side = rings - far, rows - side
+        return lax.rem(my_z + far, rings) * rows + lax.rem(my_x + side, rows)
 
     region = lax.axis_index("blk")
     my_y = region // cores
@@ -104,19 +101,9 @@
     for neighbour in blk_neighbours:
         pl.semaphore_signal(barrier, inc=1, device_id={"blk": neighbour}, device_id_type=MESH)
 
-    order = (1, 2, 0)
-
-    def stage_copy(slot, group, head):
+    def own_block(group, head):
         column = pl.multiple_of((group * seq_count + head) * width, width)
-        return pltpu.make_async_copy(
-            qkv_ref.at[:, pl.ds(column, width)], stage.at[slot, head], stage_sem.at[slot]
-        )
-
-    for slot, group in enumerate(order):
-
-        @pl.loop(0, seq_count)
-        def _(head, slot=slot, group=group):
-            stage_copy(slot, group, head).start()
+        return qkv_ref.at[:, pl.ds(column, width)]
 
     lists = ((cur_hbm, cur_ref), (kept_list_hbm, kept_list_ref), (count_hbm, count_ref))
     list_copies = [
@@ -140,58 +127,46 @@
                 blk_sem.at[level], inc=1, device_id={"blk": neighbour}, device_id_type=MESH
             )
 
-    def staged(slot):
-        pltpu.make_async_copy(stage.at[slot], stage.at[slot], stage_sem.at[slot]).wait()
-
     tell(0)
     tell_blk(0)
 
-    buffers = (k_all, v_all, q_all)
-    sends = (k_send, v_send, q_send)
-    recvs = (k_recv, v_recv, q_recv)
-
-    def send_group(slot, nearest, farthest):
-        target, send, recv = buffers[slot], sends[slot], recvs[slot]
-        recv_mine = recv.at[me] if slot == 2 else recv
-
-        for far, side in partners:
-            if nearest <= hops(far, side) <= farthest:
-                other = place(far, side)
-                pltpu.make_async_remote_copy(
-                    src_ref=stage.at[slot, other],
-                    dst_ref=target.at[me],
-                    send_sem=send,
-                    recv_sem=recv_mine,
-                    device_id={"seq": other},
-                    device_id_type=MESH,
-                ).start()
-
-    staged(0)
-    send_group(0, 1, 1)
-    staged(1)
-    send_group(1, 1, 1)
+    def send_keys_values(distance):
+        @pl.loop(0, 2)
+        def _(slot):
+            for far, side in partners:
+                if hops(far, side) == distance:
+                    other = place(far, side)
+                    pltpu.make_async_remote_copy(
+                        src_ref=own_block(slot + 1, other),
+                        dst_ref=kv_all.at[slot, me],
+                        send_sem=kv_send.at[slot],
+                        recv_sem=kv_recv.at[slot],
+                        device_id={"seq": other},
+                        device_id_type=MESH,
+                    ).start()
+
+    send_keys_values(1)
 
     pl.semaphore_wait(level_sem.at[0], len(neighbours))
     tell(1)
-    send_group(0, 2, 2)
+    send_keys_values(2)
     pl.semaphore_wait(blk_sem.at[0], len(blk_neighbours))
     tell_blk(1)
-    send_group(1, 2, 2)
-    staged(2)
 
     kept_mine = pl.ds(region * kept_own, kept_own)
 
     pltpu.make_async_copy(kept_ref, kept_all.at[kept_mine], kept_recv).start()
-    for slot in range(3):
-        recv = recvs[slot].at[me] if slot == 2 else recvs[slot]
-        pltpu.make_async_copy(stage.at[slot, me], buffers[slot].at[me], recv).start()
+    pltpu.make_async_copy(own_block(0, me), q_all.at[me], q_recv.at[me]).start()
+    for slot in range(2):
+        pltpu.make_async_copy(
+            own_block(slot + 1, me), kv_all.at[slot, me], kv_recv.at[slot]
+        ).start()
 
     for level in range(1, reach - 1):
         pl.semaphore_wait(level_sem.at[level], len(neighbours))
         if level < reach - 2:
             tell(level + 1)
-        send_group(0, level + 2, level + 2)
-        send_group(1, level + 2, level + 2)
+        send_keys_values(level + 2)
 
     pl.semaphore_wait(blk_sem.at[1], len(blk_neighbours))
     for along, core in blk_partners:
@@ -204,13 +179,23 @@
             device_id_type=MESH,
         ).start()
 
-    send_group(2, 1, reach)
+    @pl.loop(0, seq_count - 1)
+    def _(step):
+        other = partner(step, False)
+        pltpu.make_async_remote_copy(
+            src_ref=own_block(0, other),
+            dst_ref=q_all.at[me],
+            send_sem=q_send,
+            recv_sem=q_recv.at[me],
+            device_id={"seq": other},
+            device_id_type=MESH,
+        ).start()
 
     for copy in list_copies:
         copy.wait()
-    pltpu.make_async_copy(k_all, k_all, k_recv).wait()
+    pltpu.make_async_copy(kv_all.at[0], kv_all.at[0], kv_recv.at[0]).wait()
     pltpu.make_async_copy(kept_all, kept_all, kept_recv).wait()
-    pltpu.make_async_copy(v_all, v_all, v_recv).wait()
+    pltpu.make_async_copy(kv_all.at[1], kv_all.at[1], kv_recv.at[1]).wait()
 
     columns_mine = pl.ds(pl.multiple_of(me * width, width), width)
 
@@ -228,7 +213,7 @@
 
     @pl.loop(0, seq_count)
     def _(step):
-        tile = source(step)
+        tile = partner(step, True)
         pltpu.make_async_copy(q_all.at[tile], q_all.at[tile], q_recv.at[tile]).wait()
         row = tile * blk_count + region
         queries = q_all[tile]
@@ -238,7 +223,7 @@
             first = 2 * pair
             if first < near_count:
                 ids = [cur_ref[first + n, row] // blk_count for n in range(2)]
-                keys = [k_all[i] for i in ids]
+                keys = [kv_all[0, i] for i in ids]
             else:
                 slots = [first - near_count + n for n in range(2)]
                 keys = [kept_all[kept_list_ref[w, row], 0] for w in slots]
@@ -265,7 +250,7 @@
             rounded = weight.astype(jnp.bfloat16)
             if first < near_count:
                 ids = [cur_ref[first + n, row] // blk_count for n in range(2)]
-                values = [v_all[i] for i in ids]
+                values = [kv_all[1, i] for i in ids]
             else:
                 slots = [first - near_count + n for n in range(2)]
                 values = [kept_all[kept_list_ref[w, row], 1] for w in slots]
@@ -278,17 +263,16 @@
 
         @pl.when(step > 0)
         def _():
-            send_out(source(step - 1))
-
-    own_copy = pltpu.make_async_copy(mixed.at[me], out_ref.at[:, columns_mine], o_recv)
-    own_copy.start()
+            send_out(partner(step - 1, True))
+
+    out_ref[:, columns_mine] = mixed[me]
 
     others = pl.ds(0, seq_count - 1)
-    for send in sends + (o_send,):
-        pltpu.make_async_copy(k_all.at[others], k_all.at[others], send).wait()
+    for send in (kv_send.at[0], kv_send.at[1], q_send, o_send):
+        pltpu.make_async_copy(q_all.at[others], q_all.at[others], send).wait()
     kept_others = pl.ds(0, kept_own * (blk_count - 1))
     pltpu.make_async_copy(kept_all.at[kept_others], kept_all.at[kept_others], kept_send).wait()
-    pltpu.make_async_copy(out_ref, out_ref, o_recv).wait()
+    pltpu.make_async_copy(q_all.at[others], q_all.at[others], o_recv).wait()
 
 
 def per_device(qkv, kept_kv, cur_list, kept_list, kept_count):
@@ -310,26 +294,21 @@
             pltpu.SMEM(cur_list.shape[::-1], jnp.int32),
             pltpu.SMEM(kept_list.shape[::-1], jnp.int32),
             pltpu.SMEM(kept_count.shape, jnp.int32),
-            pltpu.VMEM((3, seq_count) + block, jnp.bfloat16),
             pltpu.VMEM((seq_count,) + block, jnp.bfloat16),
-            pltpu.VMEM((seq_count,) + block, jnp.bfloat16),
-            pltpu.VMEM((seq_count,) + block, jnp.bfloat16),
+            pltpu.VMEM((2, seq_count) + block, jnp.bfloat16),
             pltpu.VMEM((kept_kv.shape[0] * blk_count, 2) + block, jnp.bfloat16),
             pltpu.VMEM((tile_len, (near_count + window) * width), jnp.float32),
             pltpu.VMEM((seq_count,) + block, jnp.bfloat16),
             dma((3,)),
-            dma((3,)),
-            dma,
-            dma,
-            dma,
-            dma,
+            dma,
+            dma,
+            dma((2,)),
+            dma((2,)),
             dma,
             dma((seq_count,)),
             dma,
             dma,
-            dma,
-            dma,
-            pltpu.SemaphoreType.REGULAR((seq_count // 8 + 1,)),
+            pltpu.SemaphoreType.REGULAR((5,)),
             pltpu.SemaphoreType.REGULAR((2,)),
         ],
         compiler_params=pltpu.CompilerParams(

time: 101 us -> 101 us (level)
  no operation moved by 1% of the time
where the time goes in v6:
time: 101 us
  Pallas kernels  100 us (99%)
    pallas_call x1, Pallas kernels, per_device(): pl.pallas_call(functools.partial(kernel, seq_count, blk_count, 4, 2), out...  100 us

profile of v6, /device:TPU:2, one launch (start us, length us, event | category | flops | bytes accessed | tf_op | source)
XLA Modules:
  0.0 101.3 jit_solution(18382414258315258868)
XLA Ops:
  0.0 100.4 %shard_map.55 = bf16[128,4096]{1,0:T(8,128)(2,1)S(1)} custom-call(s32[8,256]{1,0:T(8,128)} %bitcast.3, s32[12,256]{1,0:T(8,128)} %bitcast.2, s32[256]{0:T(256)} %count_hbm.1, bf16[128,12288]{1,0:T(8,128)(2,1)} %qkv_ref.1, bf16[4,2,128,128]{3,2,1,0:T(8,128)(2,1)} %kept_ref.1), custom_call_target="tpu_custom_call" | custom-call | tf_op jit(solution)/shard_map/pallas_call | solution.py:288
  100.4 1.0 copy.7

commit v7 on v6

--- a/solution.py
+++ b/solution.py
@@ -63,7 +63,11 @@
     for far in range(rings // 2 - 1, 0, -1):
         turns += [far, rings - far]
     turns += [0]
-    partners = [(far, side % rows) for side in range(1, rows + 1) for far in turns]
+    sides = [rows // 2]
+    for side in range(rows // 2 - 1, 0, -1):
+        sides += [side, rows - side]
+    sides += [0]
+    partners = [(far, side) for side in sides for far in turns]
     partners.remove((0, 0))
     reach = rings // 2 + rows // 2
     neighbours = [place(far, side) for far, side in partners if hops(far, side) == 1]
@@ -71,7 +75,8 @@
     def partner(step, back):
         turn = lax.rem(step, rings)
         far = (turn + 1) // 2 * (1 - 2 * lax.rem(turn, 2)) + rings // 2
-        side = lax.rem(step // rings + 1, rows)
+        group = step // rings
+        side = (group + 1) // 2 * (1 - 2 * lax.rem(group, 2)) + rows // 2
         if back:
             far, side = rings - far, rows - side
         return lax.rem(my_z + far, rings) * rows + lax.rem(my_x + side, rows)

time: 101 us -> 101 us (level)
  no operation moved by 1% of the time
where the time goes in v7:
time: 101 us
  Pallas kernels  100 us (99%)
    pallas_call x1, Pallas kernels, per_device(): pl.pallas_call(functools.partial(kernel, seq_count, blk_count, 4, 2), out...  100 us

profile of v7, /device:TPU:2, one launch (start us, length us, event | category | flops | bytes accessed | tf_op | source)
XLA Modules:
  0.0 101.3 jit_solution(15267688806552092358)
XLA Ops:
  0.0 100.4 %shard_map.55 = bf16[128,4096]{1,0:T(8,128)(2,1)S(1)} custom-call(s32[8,256]{1,0:T(8,128)} %bitcast.3, s32[12,256]{1,0:T(8,128)} %bitcast.2, s32[256]{0:T(256)} %count_hbm.1, bf16[128,12288]{1,0:T(8,128)(2,1)} %qkv_ref.1, bf16[4,2,128,128]{3,2,1,0:T(8,128)(2,1)} %kept_ref.1), custom_call_target="tpu_custom_call" | custom-call | tf_op jit(solution)/shard_map/pallas_call | solution.py:293
  100.4 1.0 copy.7
